TPU v7x, 32 devices: a whole 2x2x4 slice. The times are simulated.
32 devices in a mesh: seg: 8 (over z, x), head: 4 (over y, core).
Axes of the slice: x: 2, y: 2, z: 4, core: 2. Of those that a mesh axis runs over, the one named last changes fastest.
Arguments:
- q_heads: bfloat16 [6144, 2048], P('seg', 'head'), may hold values from -6 to 6
- k_heads: bfloat16 [6144, 2048], P('seg', 'head'), may hold values from -6 to 6
- v_heads: bfloat16 [6144, 2048], P('seg', 'head'), may hold values from -600 to 600
- log_decay: float32 [16, 6144], P('head', 'seg'), may hold values from -1 to 0
- parent: int32 [8], replicated, may hold values from -1 to 7, as said below
- norm_gain: float32 [2048], P('head'), may hold values from 0.1 to 1.9
- w_out: bfloat16 [2048, 6144], P('head'), may hold values from -0.125 to 0.125
Outputs:
- mixed: bfloat16 [6144, 6144], P(('seg', 'head'))
Inputs may be any that keep to these rules, and one draw needn't show every extreme that they name: A segment's parent is a root or a segment whose parent is a root; the tree has three levels, and the third is never empty.
All inputs are finite; a program needn't handle non-finite values.
Results may differ from a plain program's by a relative error of at most 0.0051.
Values sent between devices are 32-bit elements; how exact they have to be, the bound alone decides.
A program may use at most 128 MiB of HBM per device.

v0:
```python
import jax
import jax.numpy as jnp
from jax import lax
from jax.sharding import PartitionSpec as P


def per_device(q_heads, k_heads, v_heads, log_decay, parent, norm_gain, w_out):
    segment_len = q_heads.shape[0]
    head_count = log_decay.shape[0]
    head_width = q_heads.shape[1] // head_count
    queries = q_heads.reshape(segment_len, head_count, head_width)
    key_rows = k_heads.reshape(segment_len, head_count, head_width)
    values = v_heads.reshape(segment_len, head_count, head_width)
    running = jnp.cumsum(log_decay, axis=1)
    segment_total = running[:, -1]
    key_weight = jnp.exp(segment_total[:, None] - running)
    weighted = key_rows.astype(jnp.float32) * key_weight.T[:, :, None]
    local_state = jnp.einsum(
        "shd,she->hde", weighted, values.astype(jnp.float32), precision=lax.Precision.HIGHEST
    )
    scores = jnp.einsum("thd,shd->hts", queries, key_rows, preferred_element_type=jnp.float32)
    row_index = lax.broadcasted_iota(jnp.int32, (segment_len, segment_len), 0)
    col_index = lax.broadcasted_iota(jnp.int32, (segment_len, segment_len), 1)
    causal = row_index >= col_index
    log_gap = running[:, :, None] - running[:, None, :]
    decay_factor = jnp.where(causal[None], jnp.exp(jnp.minimum(log_gap, 0.0)), 0.0)
    weights = (scores * head_width ** (-0.5) * decay_factor).astype(jnp.bfloat16)
    within = jnp.einsum("hts,she->the", weights, values, preferred_element_type=jnp.float32)
    own_index = lax.axis_index("seg")
    parent_id = parent[own_index]
    grand_id = jnp.where(parent_id >= 0, parent[jnp.maximum(parent_id, 0)], -1)
    states = lax.all_gather(local_state[None], "seg", axis=0, tiled=True)
    totals = lax.all_gather(segment_total[None], "seg", axis=0, tiled=True)
    segment_ids = jnp.arange(states.shape[0], dtype=jnp.int32)
    is_parent = segment_ids == parent_id
    is_grand = segment_ids == grand_id
    parent_sum = jnp.sum(jnp.where(is_parent[:, None, None, None], states, 0.0), axis=0)
    grand_sum = jnp.sum(jnp.where(is_grand[:, None, None, None], states, 0.0), axis=0)
    parent_total = jnp.sum(jnp.where(is_parent[:, None], totals, 0.0), axis=0)
    parent_sum, grand_sum, parent_total = (parent_sum, grand_sum, parent_total)
    prefix = jnp.exp(parent_total)[:, None, None] * grand_sum + parent_sum
    prefix_term = (
        jnp.einsum(
            "thd,hde->the", queries.astype(jnp.float32), prefix, precision=lax.Precision.HIGHEST
        )
        * jnp.exp(running).T[:, :, None]
    )
    attention = (prefix_term + within).reshape(segment_len, head_count * head_width)
    squares = lax.psum(jnp.sum(attention * attention, axis=1), "head")
    total_features = head_count * head_width * lax.axis_size("head")
    inverse = 1.0 / jnp.sqrt(squares / total_features + 1e-06)
    normed = (attention * inverse[:, None] * norm_gain[None, :]).astype(jnp.bfloat16)
    mixed = lax.psum_scatter(
        jnp.dot(normed, w_out, preferred_element_type=jnp.float32),
        "head",
        scatter_dimension=0,
        tiled=True,
    )
    return mixed.astype(jnp.bfloat16)


def solution(mesh):
    return jax.shard_map(
        per_device,
        mesh=mesh,
        in_specs=(
            P("seg", "head"),
            P("seg", "head"),
            P("seg", "head"),
            P("head", "seg"),
            P(),
            P("head"),
            P("head", None),
        ),
        out_specs=P(("seg", "head"), None),
        check_vma=False,
    )
```

profile of v0, /device:TPU:0, one launch (start us, length us, event | category | flops | bytes accessed | tf_op | source)
XLA Modules:
  0.0 234.6 jit_solution(15167253058687618074)
XLA Ops:
  6.5 0.8 reshape.72
  7.3 1.1 reduce-window.6
  8.5 0.2 slice_reduce_fusion
  8.6 0.2 reduce-window.9
  8.8 0.1 add_bitcast_fusion
  8.9 0.2 slice_reduce_fusion.1
  9.1 0.1 exponential_bitcast_fusion.1
  9.2 0.0 copy-start.4
  9.2 1.4 copy.31
  10.6 1.4 copy.32
  12.0 1.7 fusion.6
  13.7 0.0 all-gather.4.cloned.1.call-update
  13.7 0.0 reduce-scatter.2.cloned.1.call-start
  13.8 0.6 dynamic_slice.6
  15.7 0.6 dynamic_slice.7
  16.2 0.6 dynamic-slice
  17.5 0.2 dynamic-update-slice
  17.7 23.5 %all-reduce = f32[32]{0:T(128)S(1)} all-reduce(f32[32]{0:T(128)S(1)} %dynamic-update-slice), channel_id=2, replica_groups=mesh['seg'=8,'head'=4] {'seg'}, use_global_device_ids=true, to_apply=%add | all-reduce | flops 32 | bytes 256
  41.2 0.1 reshape.78
  41.3 0.7 iota_compare_fusion.2
  41.9 0.1 select_reduce_fusion.2
  42.6 0.2 iota_compare_fusion
  42.8 5.6 %fusion = f32[4,768,128]{1,2,0:T(8,128)} fusion(bf16[768,4,128]{0,2,1:T(8,128)(2,1)S(1)} %bitcast.52, f32[4,768]{1,0:T(4,128)S(1)} %get-tuple-element.8, pred[768,768]{1,0:T(8,128)(4,1)S(1)} %iota_compare_fusion, bf16[768,4,128]{0,2,1:T(8,128)(2,1)S(1)} %bitcast.50, bf16[768,512]{1,0:T(8,128)(2,1)S(1)} %copy-done), kind=kOutput, calls=%fused_computation.1 | convolution fusion | flops 1222115328 | bytes 4534272 | tf_op jit(solution)/shard_map/hts,she->the/dot_general | solution.py:28
  48.3 17.5 %all-gather.4.cloned.1.call-done = f32[32,128,128]{2,1,0:T(8,128)} async-done(((f32[4,128,128]{2,1,0:T(8,128)}), f32[32,128,128]{2,1,0:T(8,128)}) %all-gather.4.cloned.1.call-update) | async-done | bytes 2097168 | tf_op jit(solution)/shard_map/all_gather | solution.py:32
  65.9 2.1 select_reduce_fusion.1
  68.0 1.1 multiply_reduce_fusion
  69.1 5.7 %psum.7 = f32[768]{0:T(1024)S(1)} all-reduce(f32[768]{0:T(1024)S(1)} %get-tuple-element.9), channel_id=1, replica_groups=mesh['seg'=8,'head'=4] {'head'}, use_global_device_ids=true, to_apply=%region_6.7 | all-reduce | flops 768 | bytes 6144 | tf_op jit(solution)/shard_map/psum | solution.py:49
  74.8 0.2 fusion.5
  75.0 11.9 %fusion.21 = f32[768,6144]{1,0:T(8,128)} fusion(bf16[768,512]{0,1:T(8,128)(2,1)S(1)} %fusion.5, bf16[512,6144]{1,0:T(8,128)(2,1)} %param.13), kind=kOutput, calls=%fused_computation.36 | convolution fusion | flops 4831838208 | bytes 25952256 | tf_op jit(solution)/shard_map/dot_general | solution.py:54
  86.9 0.0 reduce-scatter.2.cloned.1.call-update
  87.0 136.8 %reduce-scatter.2.cloned.1.call-done = f32[192,6144]{1,0:T(8,128)} async-done(((f32[768,6144]{1,0:T(8,128)}), f32[192,6144]{1,0:T(8,128)}) %reduce-scatter.2.cloned.1.call-update) | async-done | bytes 4718608 | tf_op jit(solution)/shard_map/reduce_scatter | solution.py:53
  223.7 4.1 %convert_element_type.17 = bf16[192,6144]{1,0:T(8,128)(2,1)} convert(f32[192,6144]{1,0:T(8,128)} %reduce-scatter.2.cloned.1.call-done) | non-fusion elementwise | flops 1179648 | bytes 7077888 | tf_op jit(solution)/shard_map/convert_element_type | solution.py:59
  (15 shorter events, 0.1 us)
Async XLA Ops:
  6.5 36.2 %copy-start = (bf16[768,512]{1,0:T(8,128)(2,1)S(1)}, bf16[768,512]{1,0:T(8,128)(2,1)}, u32[]{:S(2)}) copy-start(bf16[768,512]{1,0:T(8,128)(2,1)} %param.7) | copy-start | bytes 2359300
  6.5 59.3 %all-gather.4.cloned.1.call-start = ((), (), s32[]{:S(2)}) async-start(), calls=%async_computation.2 | async-start | bytes 2359296 | tf_op jit(solution)/shard_map/all_gather | solution.py:32
  9.2 4.6 %copy-start.3 = (s32[8]{0:T(128)S(1)}, s32[8]{0:T(128)}, u32[]{:S(2)}) copy-start(s32[8]{0:T(128)} %param.11) | copy-start | bytes 100
  9.2 7.1 %copy-start.4 = (u32[32]{0:T(128)S(1)}, u32[32]{0:T(128)}, u32[]{:S(2)}) copy-start(u32[32]{0:T(128)} %constant.29) | copy-start | bytes 388
  13.7 210.0 %reduce-scatter.2.cloned.1.call-start = ((), (), s32[]{:S(2)}) async-start(), calls=%async_computation.1 | async-start | bytes 23592960 | tf_op jit(solution)/shard_map/reduce_scatter | solution.py:53
  65.9 2.1 copy-start.1
  68.0 6.8 %copy-start.2 = (f32[512]{0:T(512)S(1)}, f32[512]{0:T(512)}, u32[]{:S(2)}) copy-start(f32[512]{0:T(512)} %param.12) | copy-start | bytes 6148
Sparse Core Ops, SparseCore 0:
  13.8 51.9 all-gather.3
  87.1 136.6 reduce-scatter.1
where the time goes:
time: 235 us
  waiting for transfers between devices  154 us (66%)
  blocking collectives  29.1 us (12%)
  matrix products  20.2 us (9%)
  between operations  16 us (7%)
  other arithmetic  8.75 us (4%)
  local copies, waits for them, and re-layouts  6.08 us (3%)
    reduce_scatter x1, waiting for transfers between devices, per_device(): lax.psum_scatter(jnp.dot(normed, w_out, preferred_element_type=jnp.float3...  137 us
    unnamed x1, blocking collectives  23.5 us
    all_gather x1, waiting for transfers between devices, per_device(): states = lax.all_gather(local_state[None], 'seg', axis=0, tiled=True)  17.5 us
    dot_general x1, matrix products, per_device(): jnp.dot(normed, w_out, preferred_element_type=jnp.float32)  11.9 us
    psum x1, blocking collectives, per_device(): squares = lax.psum(jnp.sum(attention * attention, axis=1), 'head')  5.67 us
    dot_general x1, matrix products, per_device(): jnp.einsum('hts,she->the', weights, values, preferred_element_type=jnp.fl...  5.55 us
  transfers between devices with their start and end apart: 2, of which 2 were waited for; matrix products, arithmetic and copies ran while one was open for 4% of the time, Pallas kernels for 0%

commit v1 on v0

--- a/solution.py
+++ b/solution.py
@@ -2,6 +2,28 @@
 import jax.numpy as jnp
 from jax import lax
 from jax.sharding import PartitionSpec as P
+
+
+def switch_joints_on_mesh(m):
+    outer, near, o_now = (lax.axis_size("seg"), lax.axis_index("seg"), m.shape[0])
+    steps_seen = [c * outer if to_i == 0 else c for to_i, c in enumerate(m.shape)]
+    g_now = lax.dynamic_update_slice_in_dim(jnp.zeros(steps_seen, m.dtype), m, near * o_now, axis=0)
+    long_array = inter = m
+    for kk in range(1, outer // 2 + 1):
+        long_array = lax.ppermute(
+            long_array, axis_name="seg", perm=[(to_i, (to_i + 1) % outer) for to_i in range(outer)]
+        )
+        g_now = lax.dynamic_update_slice_in_dim(
+            g_now, long_array, (near - kk) % outer * o_now, axis=0
+        )
+        if 2 * kk < outer:
+            inter = lax.ppermute(
+                inter, "seg", [(to_i, (to_i - 1) % outer) for to_i in range(outer)]
+            )
+            g_now = lax.dynamic_update_slice_in_dim(
+                g_now, inter, (near + kk) % outer * o_now, axis=0
+            )
+    return g_now
 
 
 def per_device(q_heads, k_heads, v_heads, log_decay, parent, norm_gain, w_out):
@@ -29,7 +51,7 @@
     own_index = lax.axis_index("seg")
     parent_id = parent[own_index]
     grand_id = jnp.where(parent_id >= 0, parent[jnp.maximum(parent_id, 0)], -1)
-    states = lax.all_gather(local_state[None], "seg", axis=0, tiled=True)
+    states = switch_joints_on_mesh(local_state[None])
     totals = lax.all_gather(segment_total[None], "seg", axis=0, tiled=True)
     segment_ids = jnp.arange(states.shape[0], dtype=jnp.int32)
     is_parent = segment_ids == parent_id

time: 235 us -> 248 us (1.055)
  starting transfers between devices: 0.04 us -> 13 us
  local copies, waits for them, and re-layouts: 6.08 us -> 10.3 us
  blocking collectives: 29.1 us -> 25.9 us
    all_gather x1 -> x0, waiting for transfers between devices: 17.5 us -> none  [per_device(): states = lax.all_gather(local_state[None], 'seg', axis=0, tiled=True)]
    ppermute x0 -> x7, waiting for transfers between devices: none -> 16 us  [the longest x3 12.3 us: switch_joints_on_mesh(): lax.ppermute(inter, 'seg', [(to_i, (to_i - 1) % outer) for to_i in range(...]
    ppermute x0 -> x7, starting transfers between devices: none -> 13 us  [the longest x4 9.86 us: switch_joints_on_mesh(): lax.ppermute(long_array, axis_name='seg', perm=[(to_i, (to_i + 1) % outer...]
    unnamed x1, blocking collectives: 23.5 us -> 20.2 us
  transfers between devices with their start and end apart: 2 -> 8, of which waited for: 2 -> 6; matrix products, arithmetic and copies ran while one was open for 4% -> 5% of each run, Pallas kernels for 0% -> 0%
where the time goes in v1:
time: 248 us; the launch traced here: 247 us
  waiting for transfers between devices  153 us (62%)
  blocking collectives  25.9 us (10%)
  matrix products  21.6 us (9%)
  between operations  16.4 us (7%)
  starting transfers between devices  13 us (5%)
  local copies, waits for them, and re-layouts  10.3 us (4%)
  other arithmetic  7.03 us (3%)
    reduce_scatter x1, waiting for transfers between devices, per_device(): lax.psum_scatter(jnp.dot(normed, w_out, preferred_element_type=jnp.float3...  137 us
    unnamed x1, blocking collectives  20.2 us
    ppermute x3, waiting for transfers between devices, switch_joints_on_mesh(): lax.ppermute(inter, 'seg', [(to_i, (to_i - 1) % outer) for to_i in range(...  12.3 us
    dot_general x1, matrix products, per_device(): jnp.dot(normed, w_out, preferred_element_type=jnp.float32)  11.9 us
    ppermute x4, starting transfers between devices, switch_joints_on_mesh(): lax.ppermute(long_array, axis_name='seg', perm=[(to_i, (to_i + 1) % outer...  9.86 us
    dot_general x1, matrix products, per_device(): jnp.einsum('hts,she->the', weights, values, preferred_element_type=jnp.fl...  6.95 us
    psum x1, blocking collectives, per_device(): squares = lax.psum(jnp.sum(attention * attention, axis=1), 'head')  5.67 us
  transfers between devices with their start and end apart: 8, of which 6 were waited for; matrix products, arithmetic and copies ran while one was open for 5% of the time, Pallas kernels for 0%

profile of v1, /device:TPU:0, one launch (start us, length us, event | category | flops | bytes accessed | tf_op | source)
XLA Modules:
  0.0 247.1 jit_solution(16930334126921008035)
XLA Ops:
  6.5 0.8 reshape.72
  7.4 1.1 reduce-window.6
  9.2 2.3 copy.31
  11.5 1.2 copy.32
  12.7 0.2 broadcast_in_dim.58
  12.9 0.9 copy-done.1
  13.8 0.2 copy-done.2
  14.1 1.6 constant_dynamic-update-slice_fusion.7
  15.7 3.0 %collective-permute-start = (f32[1,4,128,128]{3,2,1,0:T(8,128)}, f32[1,4,128,128]{3,2,1,0:T(8,128)}, u32[]{:S(2)}, u32[]{:S(2)}) collective-permute-start(f32[1,4,128,128]{3,2,1,0:T(8,128)} %get-tuple-element.10), channel_id=1, source_target_pairs={{0,4},{4,8},{8,12},{12,16},{16,20},{20,24},{24,28},{28,0},{1,5},{5... | collective-permute-start | bytes 786440 | tf_op jit(solution)/shard_map/ppermute | solution.py:13
  18.6 3.0 %collective-permute-start.1 = (f32[1,4,128,128]{3,2,1,0:T(8,128)}, f32[1,4,128,128]{3,2,1,0:T(8,128)}, u32[]{:S(2)}, u32[]{:S(2)}) collective-permute-start(f32[1,4,128,128]{3,2,1,0:T(8,128)} %get-tuple-element.10), channel_id=1, source_target_pairs={{0,28},{4,0},{8,4},{12,8},{16,12},{20,16},{24,20},{28,24},{1,29},{... | collective-permute-start | bytes 786440 | tf_op jit(solution)/shard_map/ppermute | solution.py:20
  21.9 6.9 %fusion = f32[4,768,128]{1,2,0:T(8,128)} fusion(bf16[768,4,128]{0,2,1:T(8,128)(2,1)} %bitcast.52, f32[4,768]{1,0:T(4,128)S(1)} %get-tuple-element.8, pred[768,768]{1,0:T(8,128)(4,1)S(1)} %iota_compare_fusion, bf16[768,4,128]{0,2,1:T(8,128)(2,1)} %bitcast.50, bf16[768,512]{1,0:T(8,128)(2,1)S(1)} %copy-done), kind=kOutput, calls=%fused_computation.1 | convolution fusion | flops 1222115328 | bytes 4534272 | tf_op jit(solution)/shard_map/hts,she->the/dot_general | solution.py:50
  28.9 0.7 dynamic_slice.6
  29.5 0.6 collective-permute-done
  30.1 2.5 %collective-permute-start.2 = (f32[1,4,128,128]{3,2,1,0:T(8,128)}, f32[1,4,128,128]{3,2,1,0:T(8,128)S(1)}, u32[]{:S(2)}, u32[]{:S(2)}) collective-permute-start(f32[1,4,128,128]{3,2,1,0:T(8,128)} %collective-permute-done), channel_id=1, source_target_pairs={{0,4},{4,8},{8,12},{12,16},{16,20},{20,24},{24,28},{28,0},{1,5},{5... | collective-permute-start | bytes 786440 | tf_op jit(solution)/shard_map/ppermute | solution.py:13
  32.6 0.7 iota_compare_fusion.2
  34.7 0.7 dynamic_slice.7
  35.4 0.6 dynamic-slice
  36.5 0.2 dynamic-update-slice
  36.8 20.2 %all-reduce = f32[32]{0:T(128)S(1)} all-reduce(f32[32]{0:T(128)S(1)} %dynamic-update-slice), channel_id=2, replica_groups=mesh['seg'=8,'head'=4] {'seg'}, use_global_device_ids=true, to_apply=%add | all-reduce | flops 32 | bytes 256
  58.1 1.9 collective-permute-start.4
  60.1 1.0 constant_dynamic-update-slice_fusion.6
  61.0 1.0 constant_dynamic-update-slice_fusion.5
  62.0 8.7 %collective-permute-done.3 = f32[1,4,128,128]{3,2,1,0:T(8,128)S(1)} collective-permute-done((f32[1,4,128,128]{3,2,1,0:T(8,128)}, f32[1,4,128,128]{3,2,1,0:T(8,128)S(1)}, u32[]{:S(2)}, u32[]{:S(2)}) %collective-permute-start.3) | collective-permute-done | bytes 262176 | tf_op jit(solution)/shard_map/ppermute | solution.py:20
  70.9 2.5 %collective-permute-start.6 = (f32[1,4,128,128]{3,2,1,0:T(8,128)S(1)}, f32[1,4,128,128]{3,2,1,0:T(8,128)S(1)}, u32[]{:S(2)}, u32[]{:S(2)}) collective-permute-start(f32[1,4,128,128]{3,2,1,0:T(8,128)S(1)} %collective-permute-done.4), channel_id=1, source_target_pairs={{0,4},{4,8},{8,12},{12,16},{16,20},{20,24},{24,28},{28,0},{1,5},{5... | collective-permute-start | bytes 786440 | tf_op jit(solution)/shard_map/ppermute | solution.py:13
  73.4 3.6 %collective-permute-done.5 = f32[1,4,128,128]{3,2,1,0:T(8,128)S(1)} collective-permute-done((f32[1,4,128,128]{3,2,1,0:T(8,128)S(1)}, f32[1,4,128,128]{3,2,1,0:T(8,128)S(1)}, u32[]{:S(2)}, u32[]{:S(2)}) %collective-permute-start.5) | collective-permute-done | bytes 262176 | tf_op jit(solution)/shard_map/ppermute | solution.py:20
  77.1 2.8 %collective-permute-done.6 = f32[1,4,128,128]{3,2,1,0:T(8,128)S(1)} collective-permute-done((f32[1,4,128,128]{3,2,1,0:T(8,128)S(1)}, f32[1,4,128,128]{3,2,1,0:T(8,128)S(1)}, u32[]{:S(2)}, u32[]{:S(2)}) %collective-permute-start.6) | collective-permute-done | bytes 262176 | tf_op jit(solution)/shard_map/ppermute | solution.py:13
  80.0 0.4 select_reduce_fusion.1
  80.4 1.1 multiply_reduce_fusion
  81.5 5.7 %psum.7 = f32[768]{0:T(1024)S(1)} all-reduce(f32[768]{0:T(1024)S(1)} %get-tuple-element.11), channel_id=1, replica_groups=mesh['seg'=8,'head'=4] {'head'}, use_global_device_ids=true, to_apply=%region_6.7 | all-reduce | flops 768 | bytes 6144 | tf_op jit(solution)/shard_map/psum | solution.py:71
  87.4 11.9 %fusion.24 = f32[768,6144]{1,0:T(8,128)} fusion(bf16[768,512]{0,1:T(8,128)(2,1)S(1)} %fusion.5, bf16[512,6144]{1,0:T(8,128)(2,1)} %param.13), kind=kOutput, calls=%fused_computation.45 | convolution fusion | flops 4831838208 | bytes 25952256 | tf_op jit(solution)/shard_map/dot_general | solution.py:76
  99.3 136.9 %reduce-scatter.2.cloned.1.call-done = f32[192,6144]{1,0:T(8,128)} async-done(((f32[768,6144]{1,0:T(8,128)}), f32[192,6144]{1,0:T(8,128)}) %reduce-scatter.2.cloned.1.call-update) | async-done | bytes 4718608 | tf_op jit(solution)/shard_map/reduce_scatter | solution.py:75
  236.2 4.1 %convert_element_type.17 = bf16[192,6144]{1,0:T(8,128)(2,1)} convert(f32[192,6144]{1,0:T(8,128)} %reduce-scatter.2.cloned.1.call-done) | non-fusion elementwise | flops 1179648 | bytes 7077888 | tf_op jit(solution)/shard_map/convert_element_type | solution.py:81
  (40 shorter events, 1.6 us)
Async XLA Ops:
  6.5 15.3 %copy-start = (bf16[768,512]{1,0:T(8,128)(2,1)S(1)}, bf16[768,512]{1,0:T(8,128)(2,1)}, u32[]{:S(2)}) copy-start(bf16[768,512]{1,0:T(8,128)(2,1)} %param.7) | copy-start | bytes 2359300
  6.5 5.0 %copy-start.4 = (bf16[768,512]{1,0:T(8,128)(2,1)S(1)}, bf16[768,512]{1,0:T(8,128)(2,1)}, u32[]{:S(2)}) copy-start(bf16[768,512]{1,0:T(8,128)(2,1)} %param.9) | copy-start | bytes 2359300
  6.5 229.6 %reduce-scatter.2.cloned.1.call-start = ((), (), s32[]{:S(2)}) async-start(), calls=%async_computation.1 | async-start | bytes 23592960 | tf_op jit(solution)/shard_map/reduce_scatter | solution.py:75
  12.7 1.1 copy-start.1
  12.7 1.4 copy-start.2
  15.7 14.5 %collective-permute-start = (f32[1,4,128,128]{3,2,1,0:T(8,128)}, f32[1,4,128,128]{3,2,1,0:T(8,128)}, u32[]{:S(2)}, u32[]{:S(2)}) collective-permute-start(f32[1,4,128,128]{3,2,1,0:T(8,128)} %get-tuple-element.10), channel_id=1, source_target_pairs={{0,4},{4,8},{8,12},{12,16},{16,20},{20,24},{24,28},{28,0},{1,5},{5... | collective-permute-start | bytes 786440 | tf_op jit(solution)/shard_map/ppermute | solution.py:13
  18.6 39.2 %collective-permute-start.1 = (f32[1,4,128,128]{3,2,1,0:T(8,128)}, f32[1,4,128,128]{3,2,1,0:T(8,128)}, u32[]{:S(2)}, u32[]{:S(2)}) collective-permute-start(f32[1,4,128,128]{3,2,1,0:T(8,128)} %get-tuple-element.10), channel_id=1, source_target_pairs={{0,28},{4,0},{8,4},{12,8},{16,12},{20,16},{24,20},{28,24},{1,29},{... | collective-permute-start | bytes 786440 | tf_op jit(solution)/shard_map/ppermute | solution.py:20
  21.9 7.0 %copy-start.6 = (s32[8]{0:T(128)S(1)}, s32[8]{0:T(128)}, u32[]{:S(2)}) copy-start(s32[8]{0:T(128)} %param.11) | copy-start | bytes 100
  21.9 13.5 %copy-start.7 = (u32[32]{0:T(128)S(1)}, u32[32]{0:T(128)}, u32[]{:S(2)}) copy-start(u32[32]{0:T(128)} %constant.78) | copy-start | bytes 388
  30.1 28.0 %collective-permute-start.2 = (f32[1,4,128,128]{3,2,1,0:T(8,128)}, f32[1,4,128,128]{3,2,1,0:T(8,128)S(1)}, u32[]{:S(2)}, u32[]{:S(2)}) collective-permute-start(f32[1,4,128,128]{3,2,1,0:T(8,128)} %collective-permute-done), channel_id=1, source_target_pairs={{0,4},{4,8},{8,12},{12,16},{16,20},{20,24},{24,28},{28,0},{1,5},{5... | collective-permute-start | bytes 786440 | tf_op jit(solution)/shard_map/ppermute | solution.py:13
  57.9 12.8 %collective-permute-start.3 = (f32[1,4,128,128]{3,2,1,0:T(8,128)}, f32[1,4,128,128]{3,2,1,0:T(8,128)S(1)}, u32[]{:S(2)}, u32[]{:S(2)}) collective-permute-start(f32[1,4,128,128]{3,2,1,0:T(8,128)} %collective-permute-done.1), channel_id=1, source_target_pairs={{0,28},{4,0},{8,4},{12,8},{16,12},{20,16},{24,20},{28,24},{1,29},{... | collective-permute-start | bytes 786440 | tf_op jit(solution)/shard_map/ppermute | solution.py:20
  58.1 12.7 %collective-permute-start.4 = (f32[1,4,128,128]{3,2,1,0:T(8,128)S(1)}, f32[1,4,128,128]{3,2,1,0:T(8,128)S(1)}, u32[]{:S(2)}, u32[]{:S(2)}) collective-permute-start(f32[1,4,128,128]{3,2,1,0:T(8,128)S(1)} %collective-permute-done.2), channel_id=1, source_target_pairs={{0,4},{4,8},{8,12},{12,16},{16,20},{20,24},{24,28},{28,0},{1,5},{5... | collective-permute-start | bytes 786440 | tf_op jit(solution)/shard_map/ppermute | solution.py:13
  70.7 6.4 %collective-permute-start.5 = (f32[1,4,128,128]{3,2,1,0:T(8,128)S(1)}, f32[1,4,128,128]{3,2,1,0:T(8,128)S(1)}, u32[]{:S(2)}, u32[]{:S(2)}) collective-permute-start(f32[1,4,128,128]{3,2,1,0:T(8,128)S(1)} %collective-permute-done.3), channel_id=1, source_target_pairs={{0,28},{4,0},{8,4},{12,8},{16,12},{20,16},{24,20},{28,24},{1,29},{... | collective-permute-start | bytes 786440 | tf_op jit(solution)/shard_map/ppermute | solution.py:20
  70.9 9.1 %collective-permute-start.6 = (f32[1,4,128,128]{3,2,1,0:T(8,128)S(1)}, f32[1,4,128,128]{3,2,1,0:T(8,128)S(1)}, u32[]{:S(2)}, u32[]{:S(2)}) collective-permute-start(f32[1,4,128,128]{3,2,1,0:T(8,128)S(1)} %collective-permute-done.4), channel_id=1, source_target_pairs={{0,4},{4,8},{8,12},{12,16},{16,20},{20,24},{24,28},{28,0},{1,5},{5... | collective-permute-start | bytes 786440 | tf_op jit(solution)/shard_map/ppermute | solution.py:13
  73.4 7.0 %copy-start.3 = (f32[4,768,128]{1,2,0:T(8,128)S(1)}, f32[4,768,128]{1,2,0:T(8,128)}, u32[]{:S(2)}) copy-start(f32[4,768,128]{1,2,0:T(8,128)} %fusion) | copy-start | bytes 4718596
  80.4 6.8 %copy-start.5 = (f32[512]{0:T(512)S(1)}, f32[512]{0:T(512)}, u32[]{:S(2)}) copy-start(f32[512]{0:T(512)} %param.12) | copy-start | bytes 6148
Sparse Core Ops, SparseCore 0:
  99.4 136.6 reduce-scatter.1
